TPU v7x, 512 devices: a whole 4x4x16 slice. The times are simulated.
512 devices in a mesh: tile: 32 (over y, x, core), fsdp: 16 (over z).
Axes of the slice: x: 4, y: 4, z: 16, core: 2. Of those that a mesh axis runs over, the one named last changes fastest.
Arguments:
- images: bfloat16 [16, 32, 8, 128, 320], P('fsdp', 'tile'), may hold values from -80 to 80
- tile_rows: int32 [16, 32], P('fsdp', 'tile'), may hold values from 1 to 8, 160 in all within a row
- cotangent: bfloat16 [16, 32, 8, 128, 320], P('fsdp', 'tile'), may hold values from -6 to 6
- master_weight: float32 [2880, 320], P('fsdp'), may hold values from -0.109375 to 0.109375
- norm_gain: float32 [320], replicated, may hold values from 0.5 to 1.5
- norm_bias: float32 [320], replicated, may hold values from -3 to 3
- first_moment: float32 [2880, 320], P('fsdp'), may hold values from -6 to 6
- second_moment: float32 [2880, 320], P('fsdp'), may hold values from 0.5 to 4
Outputs:
- activation: bfloat16 [16, 32, 8, 128, 320], P('fsdp', 'tile')
- image_grad: bfloat16 [16, 32, 8, 128, 320], P('fsdp', 'tile')
- weight_grad: float32 [2880, 320], P('fsdp')
- new_weight: float32 [2880, 320], P('fsdp')
- new_first: float32 [2880, 320], P('fsdp')
- new_second: float32 [2880, 320], P('fsdp')
- gain_grad: float32 [320], replicated
- bias_grad: float32 [320], replicated
Inputs may be any that keep to these rules, and one draw needn't show every extreme that they name: `tile_rows`: in each frame the 32 counts sum to 160 and the largest is exactly 8.
All inputs are finite; a program needn't handle non-finite values. No bound on the sum of `tile_rows` on one device may be relied on, other than what follows from the above.
Results may differ from a plain program's by a relative error of at most 0.027.
Values may be sent and summed in bfloat16 or wider, within the bound.
No kernel may reach another device: no remote copies, remote signals or barrier semaphores. Data moves between devices by JAX's collectives and lax.ppermute only.
A program may use at most 64 MiB of HBM per device.

v0:
```python
import jax
import jax.numpy as jnp
from jax import lax
from jax.sharding import PartitionSpec as P

GROUPS = 32
ROWS_MEAN = 5


def extended(cells, sides, width):
    for axis, dim in sides:
        count = lax.axis_size(axis)
        ends = count - 1
        head = lax.slice_in_dim(cells, 0, width, axis=dim)
        tail = lax.slice_in_dim(cells, cells.shape[dim] - width, cells.shape[dim], axis=dim)
        cells = jnp.concatenate(
            [
                lax.ppermute(tail, axis, [(i, (i + 1) % count) for i in range(ends)]),
                cells,
                lax.ppermute(head, axis, [((i + 1) % count, i) for i in range(ends)]),
            ],
            axis=dim,
        )
    return cells


def edge_pair(source, live_count):
    first_row = source[0:1]
    last_row = lax.dynamic_slice_in_dim(source, live_count - 1, 1, 0)
    return jnp.concatenate([first_row, last_row], axis=0)


def framed(source, beside_all, live_count):
    slot_count = source.shape[0]
    zero_row = jnp.zeros_like(source[0:1])
    stacked = jnp.concatenate([beside_all[0:1], source, zero_row], axis=0)
    marker = (jnp.arange(slot_count + 2) == live_count + 1)[:, None, None]
    stacked = jnp.where(marker, beside_all[3:4], stacked)
    return jnp.pad(stacked, ((0, 0), (1, 1), (0, 0)))


def patches_of(padded, slot_count, cell_cols):
    pieces = [
        padded[row_step : row_step + slot_count, col_step : col_step + cell_cols, :]
        for row_step in range(3)
        for col_step in range(3)
    ]
    return jnp.concatenate(pieces, axis=-1).reshape(slot_count * cell_cols, -1)


def local(
    images, tile_rows, cotangent, master_weight, norm_gain, norm_bias, first_moment, second_moment
):
    slot_count, cell_cols, channels = (images.shape[2], images.shape[3], images.shape[4])
    per_group = channels // GROUPS
    tile_count = lax.axis_size("tile")
    shards = lax.axis_size("fsdp")
    population = jnp.float32(ROWS_MEAN * tile_count * cell_cols * per_group)
    live_count = tile_rows[0, 0]
    live_rows = jnp.arange(slot_count) < live_count
    cell_mask = jnp.repeat(live_rows, cell_cols).astype(jnp.float32)[:, None]

    def grouped(values):
        return jnp.sum(values.reshape(-1, GROUPS, per_group), axis=(0, 2))

    def spread(stat):
        return jnp.repeat(stat, per_group)

    source = jnp.where(live_rows[:, None, None], images[0, 0], jnp.zeros((), jnp.bfloat16))
    beside_all = extended(edge_pair(source, live_count), (("tile", 0),), 1)
    columns = patches_of(framed(source, beside_all, live_count), slot_count, cell_cols)
    gathered = lax.all_gather(master_weight.astype(jnp.bfloat16), "fsdp", axis=0, tiled=True)
    mixed = jnp.dot(columns, gathered, preferred_element_type=jnp.float32)
    group_mean = lax.psum(grouped(mixed * cell_mask), "tile") / population
    centered = (mixed - spread(group_mean)) * cell_mask
    variance = lax.psum(grouped(centered * centered), "tile") / population
    inverse = lax.rsqrt(variance + 1e-05)
    normed = (mixed - spread(group_mean)) * spread(inverse)
    shifted = normed * norm_gain + norm_bias
    gate_value = jax.nn.sigmoid(shifted)
    activation = (shifted * gate_value * cell_mask).astype(jnp.bfloat16).reshape(images.shape)
    upstream = cotangent[0, 0].reshape(-1, channels).astype(jnp.float32) * cell_mask
    dshift = upstream * gate_value * (1.0 + shifted * (1.0 - gate_value))
    scaled = dshift * norm_gain
    delta_sum, cross_sum = lax.psum((grouped(scaled), grouped(scaled * normed)), "tile")
    gain_total, bias_total = lax.psum(
        (jnp.sum(dshift * normed, axis=0), jnp.sum(dshift, axis=0)), ("tile", "fsdp")
    )
    norm_scale = jnp.float32(shards * ROWS_MEAN * tile_count * cell_cols) ** (-0.5)
    pre_grad = spread(inverse) * (
        scaled - spread(delta_sum / population) - normed * spread(cross_sum / population)
    )
    pre_grad = (pre_grad * cell_mask).astype(jnp.bfloat16)
    grad_field = pre_grad.reshape(slot_count, cell_cols, channels)
    grad_around = extended(edge_pair(grad_field, live_count), (("tile", 0),), 1)
    grad_columns = patches_of(framed(grad_field, grad_around, live_count), slot_count, cell_cols)
    flipped = (
        gathered.reshape(9, channels, channels)[::-1]
        .transpose(0, 2, 1)
        .reshape(9 * channels, channels)
    )
    image_grad = (
        (jnp.dot(grad_columns, flipped, preferred_element_type=jnp.float32) * cell_mask)
        .astype(jnp.bfloat16)
        .reshape(images.shape)
    )
    full_grad = lax.psum(
        lax.dot_general(
            columns, pre_grad, (((0,), (0,)), ((), ())), preferred_element_type=jnp.float32
        ).astype(jnp.bfloat16),
        "tile",
    )
    grad_shard = lax.psum_scatter(full_grad, "fsdp", scatter_dimension=0, tiled=True).astype(
        jnp.float32
    )
    weight_grad = grad_shard * norm_scale
    new_first = 0.9 * first_moment + 0.1 * weight_grad
    new_second = 0.999 * second_moment + 0.001 * weight_grad * weight_grad
    first_fix = new_first / (1.0 - 0.9**10)
    second_fix = new_second / (1.0 - 0.999**10)
    new_weight = master_weight - 0.01 * first_fix / (jnp.sqrt(second_fix) + 1e-08)
    return (
        activation,
        image_grad,
        weight_grad,
        new_weight,
        new_first,
        new_second,
        gain_total * norm_scale,
        bias_total * norm_scale,
    )


def solution(mesh):
    placed = (
        P("fsdp", "tile", None, None, None),
        P("fsdp", "tile"),
        P("fsdp", "tile", None, None, None),
        P("fsdp", None),
        P(),
        P(),
        P("fsdp", None),
        P("fsdp", None),
    )
    return jax.shard_map(
        local,
        mesh=mesh,
        in_specs=placed,
        out_specs=(
            P("fsdp", "tile", None, None, None),
            P("fsdp", "tile", None, None, None),
            P("fsdp", None),
            P("fsdp", None),
            P("fsdp", None),
            P("fsdp", None),
            P(),
            P(),
        ),
        check_vma=False,
    )
```

profile of v0, /device:TPU:1, one launch (start us, length us, event | category | flops | bytes accessed | tf_op | source)
XLA Modules:
  0.0 609.0 jit_solution(12582963821743056391)
XLA Ops:
  7.2 1.7 convert_bitcast_fusion
  9.7 1.2 bitcast_select_fusion
  10.9 8.8 %collective-permute-start = (bf16[1,128,320]{1,2,0:T(8,128)(2,1)S(1)}, bf16[1,128,320]{1,2,0:T(8,128)(2,1)S(1)}, u32[]{:S(2)}, u32[]{:S(2)}) collective-permute-start(bf16[1,128,320]{1,2,0:T(8,128)(2,1)S(1)} %get-tuple-element.46), channel_id=1, source_target_pairs={{16,0},{32,16},{48,32},{64,48},{80,64},{96,80},{112,96},{128,112},... | collective-permute-start | bytes 245768 | tf_op jit(solution)/shard_map/ppermute | solution.py:20
  19.7 1.9 collective-permute-start.1
  21.6 1.5 copy.30
  23.2 1.3 dynamic-slice.4
  25.2 0.2 maximum_select_fusion
  25.4 1.1 fusion.5
  26.5 1.0 slice_dynamic-update-slice_fusion.5
  27.5 1.1 fusion.6
  28.6 1.1 fusion.7
  29.7 1.0 slice_dynamic-update-slice_fusion.4
  30.7 1.1 fusion.8
  31.8 1.1 fusion.9
  32.9 1.0 slice_dynamic-update-slice_fusion.3
  33.8 1.1 fusion.10
  34.9 8.4 %copy.29 = bf16[8,128,2880]{2,1,0:T(8,128)(2,1)} copy(bf16[8,128,2880]{1,2,0:T(8,128)(2,1)} %fusion.10) | data formatting | bytes 11796480 | tf_op jit(solution)/shard_map/concatenate | solution.py:48
  43.4 37.7 %all-gather.3.cloned.1.call-done = bf16[16,180,320]{2,1,0:T(8,128)(2,1)} async-done(((bf16[1,180,320]{2,1,0:T(8,128)(2,1)}), bf16[16,180,320]{2,1,0:T(8,128)(2,1)}) %all-gather.3.cloned.1.call-update) | async-done | bytes 1843216 | tf_op jit(solution)/shard_map/all_gather | solution.py:72
  81.1 2.8 reshape.78
  83.8 5.1 multiply_reduce_fusion.3
  89.0 0.1 reduce_sum.67
  89.1 71.5 %psum.49 = f32[32]{0:T(128)S(1)} all-reduce(f32[32]{0:T(128)S(1)} %reduce_sum.67), channel_id=1, replica_groups=mesh['tile'=32,'fsdp'=16] {'tile'}, use_global_device_ids=true, to_apply=%region_2.3 | all-reduce | flops 32 | bytes 256 | tf_op jit(solution)/shard_map/psum | solution.py:74
  160.8 0.3 multiply_reduce_fusion.2
  161.3 0.1 reduce_sum.73
  161.4 62.7 %psum.50 = f32[32]{0:T(128)S(1)} all-reduce(f32[32]{0:T(128)S(1)} %reduce_sum.73), channel_id=1, replica_groups=mesh['tile'=32,'fsdp'=16] {'tile'}, use_global_device_ids=true, to_apply=%region_5.6 | all-reduce | flops 32 | bytes 256 | tf_op jit(solution)/shard_map/psum | solution.py:76
  224.1 0.1 mul.152
  224.3 3.5 multiply_reduce_fusion
  227.9 0.1 reduce_sum.90
  228.1 0.1 reduce_sum.93
  228.2 62.9 %all-reduce.5 = (f32[32]{0:T(128)S(1)}, f32[32]{0:T(128)S(1)}) all-reduce(f32[32]{0:T(128)S(1)} %reduce_sum.93, f32[32]{0:T(128)S(1)} %reduce_sum.90), channel_id=1, replica_groups=mesh['tile'=32,'fsdp'=16] {'tile'}, use_global_device_ids=true, to_apply=%region_11.12 | all-reduce | flops 64 | bytes 512 | tf_op jit(solution)/shard_map/psum | solution.py:85
  291.5 0.8 multiply_convert_fusion
  292.3 7.4 %convolution_convert_fusion = bf16[2880,320]{1,0:T(8,128)(2,1)} fusion(bf16[1024,2880]{1,0:T(8,128)(2,1)} %bitcast.60, bf16[1024,320]{0,1:T(8,128)(2,1)S(1)} %multiply_convert_fusion), kind=kOutput, calls=%fused_computation | convolution fusion | flops 1888358400 | bytes 8396800 | tf_op jit(solution)/shard_map/dot_general | solution.py:108
  299.8 0.1 copy_bitcast_fusion
  299.9 0.7 slice_bitcast_fusion
  300.5 33.6 %fusion = bf16[192,320]{1,0:T(8,128)(2,1)S(1)} fusion(bf16[2880,320]{1,0:T(8,128)(2,1)} %convolution_convert_fusion), kind=kCustom, calls=%all-reduce-scatter | all-reduce-scatter fusion | flops 983041 | bytes 1968128
  334.1 2.7 collective-permute-start.4
  336.8 0.6 constant_dynamic-slice_fusion.1
  337.5 5.1 collective-permute-start.3
  342.6 5.2 collective-permute-start.2
  347.8 100.6 %all-reduce.4 = (f32[320]{0:T(512)S(1)}, f32[320]{0:T(512)S(1)}) all-reduce(f32[320]{0:T(512)S(1)} %get-tuple-element.32, f32[320]{0:T(512)S(1)} %get-tuple-element.35), channel_id=1, replica_groups=mesh['tile'=32,'fsdp'=16] {'tile','fsdp'}, use_global_device_ids=true, to_apply=%region_15.16 | all-reduce | flops 640 | bytes 5120 | tf_op jit(solution)/shard_map/psum | solution.py:86
  448.4 0.6 broadcast_multiply_fusion
  449.0 2.2 reshape.73
  451.2 1.8 reverse_bitcast_fusion
  453.1 2.5 copy.34
  455.6 1.2 copy.38
  456.8 0.9 copy.35
  457.7 0.2 maximum_select_fusion.1
  457.9 1.1 fusion.11
  459.0 1.0 slice_dynamic-update-slice_fusion.2
  460.0 1.1 fusion.12
  461.2 1.1 fusion.13
  462.3 1.0 slice_dynamic-update-slice_fusion.1
  463.3 1.1 fusion.14
  464.3 1.1 fusion.15
  465.4 1.0 slice_dynamic-update-slice_fusion
  466.4 1.1 fusion.16
  467.5 8.6 %copy.33 = bf16[8,128,2880]{2,1,0:T(8,128)(2,1)} copy(bf16[8,128,2880]{1,2,0:T(8,128)(2,1)} %fusion.16) | data formatting | bytes 11796480 | tf_op jit(solution)/shard_map/concatenate | solution.py:48
  476.1 0.9 concatenate.16
  477.0 0.7 constant_dynamic-slice_fusion
  477.7 4.9 fusion.4
  482.7 0.1 copy.40
  482.8 0.9 copy.36
  483.8 116.3 %all-reduce.8.cloned.1.call-done = bf16[180,320]{1,0:T(8,128)(2,1)} async-done(((bf16[180,320]{1,0:T(8,128)(2,1)}), bf16[180,320]{1,0:T(8,128)(2,1)}) %all-reduce.8.cloned.1.call-update) | async-done | bytes 115216 | tf_op jit(solution)/shard_map/psum | solution.py:107
  600.1 2.0 divide_subtract_fusion
  (46 shorter events, 1.4 us)
Async XLA Ops:
  7.2 14.4 %copy-start.3 = (bf16[1,1,8,128,320]{3,4,2,1,0:T(8,128)(2,1)S(1)}, bf16[1,1,8,128,320]{3,4,2,1,0:T(8,128)(2,1)}, u32[]{:S(2)}) copy-start(bf16[1,1,8,128,320]{3,4,2,1,0:T(8,128)(2,1)} %param.10) | copy-start | bytes 1966084
  7.2 73.9 %all-gather.3.cloned.1.call-start = ((), (), s32[]{:S(2)}) async-start(), calls=%async_computation.1 | async-start | bytes 2402304 | tf_op jit(solution)/shard_map/all_gather | solution.py:72
  8.9 591.2 %all-reduce.8.cloned.1.call-start = ((), (), s32[]{:S(2)}) async-start(), calls=%async_computation | async-start | bytes 282624 | tf_op jit(solution)/shard_map/psum | solution.py:107
  10.9 14.3 %collective-permute-start = (bf16[1,128,320]{1,2,0:T(8,128)(2,1)S(1)}, bf16[1,128,320]{1,2,0:T(8,128)(2,1)S(1)}, u32[]{:S(2)}, u32[]{:S(2)}) collective-permute-start(bf16[1,128,320]{1,2,0:T(8,128)(2,1)S(1)} %get-tuple-element.46), channel_id=1, source_target_pairs={{16,0},{32,16},{48,32},{64,48},{80,64},{96,80},{112,96},{128,112},... | collective-permute-start | bytes 245768 | tf_op jit(solution)/shard_map/ppermute | solution.py:20
  19.7 5.5 collective-permute-start.1
  83.8 140.5 %copy-start.6 = (f32[320]{0:T(512)S(1)}, f32[320]{0:T(512)}, u32[]{:S(2)}) copy-start(f32[320]{0:T(512)} %param.12) | copy-start | bytes 3844
  83.8 140.5 %copy-start.7 = (f32[320]{0:T(512)S(1)}, f32[320]{0:T(512)}, u32[]{:S(2)}) copy-start(f32[320]{0:T(512)} %param.13) | copy-start | bytes 3844
  299.8 149.2 %copy-start = (bf16[16,180,320]{2,1,0:T(8,128)(2,1)S(1)}, bf16[16,180,320]{2,1,0:T(8,128)(2,1)}, u32[]{:S(2)}) copy-start(bf16[16,180,320]{2,1,0:T(8,128)(2,1)} %all-gather.3.cloned.1.call-done) | copy-start | bytes 5529604
  334.1 141.9 %collective-permute-start.4 = (bf16[180,320]{1,0:T(8,128)(2,1)S(1)}, bf16[180,320]{1,0:T(8,128)(2,1)S(1)}, u32[]{:S(2)}, u32[]{:S(2)}) collective-permute-start(bf16[180,320]{1,0:T(8,128)(2,1)S(1)} %slice.98), channel_id=1, source_target_pairs={{0,1},{1,2},{2,3},{3,4},{4,5},{5,6},{6,7},{7,8},{8,9},{9,10},{10,1... | collective-permute-start | bytes 345608
  337.5 120.2 %collective-permute-start.3 = (bf16[1,128,320]{1,2,0:T(8,128)(2,1)}, bf16[1,128,320]{1,2,0:T(8,128)(2,1)S(1)}, u32[]{:S(2)}, u32[]{:S(2)}) collective-permute-start(bf16[1,128,320]{1,2,0:T(8,128)(2,1)} %constant_dynamic-slice_fusion.1), channel_id=1, source_target_pairs={{0,16},{16,32},{32,48},{48,64},{64,80},{80,96},{96,112},{112,128},... | collective-permute-start | bytes 245768 | tf_op jit(solution)/shard_map/ppermute | solution.py:18
  342.6 115.2 %collective-permute-start.2 = (bf16[1,128,320]{1,2,0:T(8,128)(2,1)}, bf16[1,128,320]{1,2,0:T(8,128)(2,1)S(1)}, u32[]{:S(2)}, u32[]{:S(2)}) collective-permute-start(bf16[1,128,320]{1,2,0:T(8,128)(2,1)} %slice_bitcast_fusion), channel_id=1, source_target_pairs={{16,0},{32,16},{48,32},{64,48},{80,64},{96,80},{112,96},{128,112},... | collective-permute-start | bytes 245768 | tf_op jit(solution)/shard_map/ppermute | solution.py:20
  467.5 10.2 %copy-start.1 = (bf16[9,320,320]{2,1,0:T(8,128)(2,1)S(1)}, bf16[9,320,320]{2,1,0:T(8,128)(2,1)}, u32[]{:S(2)}) copy-start(bf16[9,320,320]{2,1,0:T(8,128)(2,1)} %copy.34) | copy-start | bytes 5529604
  482.6 117.5 %copy-start.2 = (f32[180,320]{1,0:T(8,128)S(1)}, f32[180,320]{1,0:T(8,128)}, u32[]{:S(2)}) copy-start(f32[180,320]{1,0:T(8,128)} %param.11) | copy-start | bytes 691204
  482.7 117.4 %copy-start.4 = (f32[180,320]{1,0:T(8,128)S(1)}, f32[180,320]{1,0:T(8,128)}, u32[]{:S(2)}) copy-start(f32[180,320]{1,0:T(8,128)} %param.14) | copy-start | bytes 691204
  482.7 117.4 %copy-start.5 = (f32[180,320]{1,0:T(8,128)S(1)}, f32[180,320]{1,0:T(8,128)}, u32[]{:S(2)}) copy-start(f32[180,320]{1,0:T(8,128)} %param.15) | copy-start | bytes 691204
Sparse Core Ops, SparseCore 0:
  10.7 70.3 all-gather.2
  477.8 122.2 all-reduce.7
where the time goes:
time: 610 us; the launch traced here: 609 us
  blocking collectives  331 us (54%)
  waiting for transfers between devices  154 us (25%)
  local copies, waits for them, and re-layouts  55.7 us (9%)
  starting transfers between devices  23.8 us (4%)
  matrix products  17.4 us (3%)
  between operations  15.7 us (3%)
  other arithmetic  11.1 us (2%)
    psum x1, waiting for transfers between devices, local(): lax.psum(lax.dot_general(columns, pre_grad, (((0,), (0,)), ((), ())), pre...  116 us
    psum x1, blocking collectives, local(): lax.psum((jnp.sum(dshift * normed, axis=0), jnp.sum(dshift, axis=0)), ('t...  101 us
    psum x1, blocking collectives, local(): group_mean = lax.psum(grouped(mixed * cell_mask), 'tile') / population  71.5 us
    psum x1, blocking collectives, local(): lax.psum((grouped(scaled), grouped(scaled * normed)), 'tile')  62.9 us
    psum x1, blocking collectives, local(): variance = lax.psum(grouped(centered * centered), 'tile') / population  62.7 us
    all_gather x1, waiting for transfers between devices, local(): lax.all_gather(master_weight.astype(jnp.bfloat16), 'fsdp', axis=0, tiled=...  37.7 us
    unnamed x1, blocking collectives  33.6 us
    unnamed x41, local copies, waits for them, and re-layouts  25.8 us
  transfers between devices with their start and end apart: 7, of which 2 were waited for; matrix products, arithmetic and copies ran while one was open for 9% of the time, Pallas kernels for 0%

commit v1 on v0

--- a/solution.py
+++ b/solution.py
@@ -69,7 +69,12 @@
     source = jnp.where(live_rows[:, None, None], images[0, 0], jnp.zeros((), jnp.bfloat16))
     beside_all = extended(edge_pair(source, live_count), (("tile", 0),), 1)
     columns = patches_of(framed(source, beside_all, live_count), slot_count, cell_cols)
-    gathered = lax.all_gather(master_weight.astype(jnp.bfloat16), "fsdp", axis=0, tiled=True)
+    gathered = jnp.concatenate(
+        lax.all_to_all(
+            jnp.stack([master_weight.astype(jnp.bfloat16)] * lax.axis_size("fsdp")), "fsdp", 0, 0
+        ),
+        axis=0,
+    )
     mixed = jnp.dot(columns, gathered, preferred_element_type=jnp.float32)
     group_mean = lax.psum(grouped(mixed * cell_mask), "tile") / population
     centered = (mixed - spread(group_mean)) * cell_mask

time: 610 us -> 658 us (1.079)
  waiting for transfers between devices: 154 us -> 186 us
  starting transfers between devices: 23.8 us -> 34.2 us
    all_to_all x0 -> x1, waiting for transfers between devices: none -> 68.2 us  [local(): lax.all_to_all(jnp.stack([master_weight.astype(jnp.bfloat16)] * lax.axis_...]
    all_gather x1 -> x0, waiting for transfers between devices: 37.7 us -> none  [local(): lax.all_gather(master_weight.astype(jnp.bfloat16), 'fsdp', axis=0, tiled=...]
    all_to_all x0 -> x1, starting transfers between devices: none -> 15.7 us  [local(): lax.all_to_all(jnp.stack([master_weight.astype(jnp.bfloat16)] * lax.axis_...]
    unnamed x41 -> x36, local copies, waits for them, and re-layouts: 25.8 us -> 23 us
where the time goes in v1:
time: 658 us; the launch traced here: 657 us
  blocking collectives  330 us (50%)
  waiting for transfers between devices  186 us (28%)
  local copies, waits for them, and re-layouts  57.9 us (9%)
  starting transfers between devices  34.2 us (5%)
  matrix products  19.2 us (3%)
  between operations  15.6 us (2%)
  other arithmetic  14 us (2%)
    psum x1, waiting for transfers between devices, local(): lax.psum(lax.dot_general(columns, pre_grad, (((0,), (0,)), ((), ())), pre...  117 us
    psum x1, blocking collectives, local(): lax.psum((jnp.sum(dshift * normed, axis=0), jnp.sum(dshift, axis=0)), ('t...  101 us
    all_to_all x1, waiting for transfers between devices, local(): lax.all_to_all(jnp.stack([master_weight.astype(jnp.bfloat16)] * lax.axis_...  68.2 us
    psum x1, blocking collectives, local(): group_mean = lax.psum(grouped(mixed * cell_mask), 'tile') / population  67.1 us
    psum x1, blocking collectives, local(): variance = lax.psum(grouped(centered * centered), 'tile') / population  62.9 us
    psum x1, blocking collectives, local(): lax.psum((grouped(scaled), grouped(scaled * normed)), 'tile')  62.9 us
    unnamed x1, blocking collectives  36 us
    unnamed x36, local copies, waits for them, and re-layouts  23 us
  transfers between devices with their start and end apart: 7, of which 2 were waited for; matrix products, arithmetic and copies ran while one was open for 9% of the time, Pallas kernels for 0%

profile of v1, /device:TPU:1, one launch (start us, length us, event | category | flops | bytes accessed | tf_op | source)
XLA Modules:
  0.0 656.9 jit_solution(14443801103932754480)
XLA Ops:
  7.2 1.0 convert_element_type.38
  8.1 1.7 stack.2
  9.8 15.7 %all-to-all-start = ((bf16[16,180,320]{2,1,0:T(8,128)(2,1)}), bf16[16,180,320]{2,1,0:T(8,128)(2,1)S(1)}, u32[]{:S(2)}, u32[]{:S(2)}) async-start(bf16[16,180,320]{2,1,0:T(8,128)(2,1)} %stack.2), calls=%async_computation | async-start | bytes 4521984 | tf_op jit(solution)/shard_map/all_to_all | solution.py:73
  26.3 1.2 bitcast_select_fusion
  27.5 2.9 collective-permute-start
  30.4 3.0 collective-permute-start.1
  33.4 2.5 copy.30
  36.0 1.3 dynamic-slice.4
  38.0 0.2 maximum_select_fusion
  38.2 1.1 fusion.5
  39.3 1.0 slice_dynamic-update-slice_fusion.5
  40.4 1.1 fusion.6
  41.5 1.1 fusion.7
  42.6 1.0 slice_dynamic-update-slice_fusion.4
  43.6 1.1 fusion.8
  44.6 1.1 fusion.9
  45.7 1.0 slice_dynamic-update-slice_fusion.3
  46.7 1.1 fusion.10
  47.8 8.4 %copy.29 = bf16[8,128,2880]{2,1,0:T(8,128)(2,1)} copy(bf16[8,128,2880]{1,2,0:T(8,128)(2,1)} %fusion.10) | data formatting | bytes 11796480 | tf_op jit(solution)/shard_map/concatenate | solution.py:48
  56.2 68.2 %all-to-all-done = bf16[16,180,320]{2,1,0:T(8,128)(2,1)S(1)} async-done(((bf16[16,180,320]{2,1,0:T(8,128)(2,1)}), bf16[16,180,320]{2,1,0:T(8,128)(2,1)S(1)}, u32[]{:S(2)}, u32[]{:S(2)}) %all-to-all-start) | async-done | bytes 1843232 | tf_op jit(solution)/shard_map/all_to_all | solution.py:73
  124.4 2.2 reshape.72
  126.7 6.8 %multiply_reduce_fusion.3 = (f32[320]{0:T(512)S(1)}, f32[1024,320]{0,1:T(8,128)}) fusion(f32[1024]{0:T(1024)S(1)} %broadcast_bitcast_fusion, bf16[1024,2880]{1,0:T(8,128)(2,1)} %bitcast.57, bf16[2880,320]{1,0:T(8,128)(2,1)} %reshape.72), kind=kOutput, calls=%fused_computation.26 | convolution fusion | flops 1888091904 | bytes 9057536 | tf_op jit(solution)/shard_map/dot_general | solution.py:78
  133.6 0.1 reduce_sum.67
  133.7 67.1 %psum.49 = f32[32]{0:T(128)S(1)} all-reduce(f32[32]{0:T(128)S(1)} %reduce_sum.67), channel_id=1, replica_groups=mesh['tile'=32,'fsdp'=16] {'tile'}, use_global_device_ids=true, to_apply=%region_2.3 | all-reduce | flops 32 | bytes 256 | tf_op jit(solution)/shard_map/psum | solution.py:79
  201.0 1.7 multiply_reduce_fusion.2
  202.8 0.1 reduce_sum.73
  202.9 62.9 %psum.50 = f32[32]{0:T(128)S(1)} all-reduce(f32[32]{0:T(128)S(1)} %reduce_sum.73), channel_id=1, replica_groups=mesh['tile'=32,'fsdp'=16] {'tile'}, use_global_device_ids=true, to_apply=%region_5.6 | all-reduce | flops 32 | bytes 256 | tf_op jit(solution)/shard_map/psum | solution.py:81
  266.0 4.2 multiply_reduce_fusion
  270.2 0.1 reduce_sum.90
  270.6 62.9 %all-reduce.5 = (f32[32]{0:T(128)S(1)}, f32[32]{0:T(128)S(1)}) all-reduce(f32[32]{0:T(128)S(1)} %reduce_sum.93, f32[32]{0:T(128)S(1)} %reduce_sum.90), channel_id=1, replica_groups=mesh['tile'=32,'fsdp'=16] {'tile'}, use_global_device_ids=true, to_apply=%region_11.12 | all-reduce | flops 64 | bytes 512 | tf_op jit(solution)/shard_map/psum | solution.py:90
  333.8 2.5 multiply_convert_fusion
  336.4 7.4 %convolution_convert_fusion = bf16[2880,320]{1,0:T(8,128)(2,1)} fusion(bf16[1024,2880]{1,0:T(8,128)(2,1)} %bitcast.58, bf16[1024,320]{0,1:T(8,128)(2,1)S(1)} %multiply_convert_fusion), kind=kOutput, calls=%fused_computation | convolution fusion | flops 1888358400 | bytes 8396800 | tf_op jit(solution)/shard_map/dot_general | solution.py:113
  343.8 0.1 copy_bitcast_fusion
  343.9 0.7 slice_bitcast_fusion
  344.6 36.0 %fusion = bf16[192,320]{1,0:T(8,128)(2,1)S(1)} fusion(bf16[2880,320]{1,0:T(8,128)(2,1)} %convolution_convert_fusion), kind=kCustom, calls=%all-reduce-scatter | all-reduce-scatter fusion | flops 983041 | bytes 1968128
  380.6 2.0 collective-permute-start.4
  382.6 0.6 constant_dynamic-slice_fusion.1
  383.3 5.3 collective-permute-start.3
  388.6 5.2 collective-permute-start.2
  393.8 101.4 %all-reduce.4 = (f32[320]{0:T(512)S(1)}, f32[320]{0:T(512)S(1)}) all-reduce(f32[320]{0:T(512)S(1)} %get-tuple-element.32, f32[320]{0:T(512)S(1)} %get-tuple-element.35), channel_id=1, replica_groups=mesh['tile'=32,'fsdp'=16] {'tile','fsdp'}, use_global_device_ids=true, to_apply=%region_15.16 | all-reduce | flops 640 | bytes 5120 | tf_op jit(solution)/shard_map/psum | solution.py:91
  495.2 0.6 broadcast_multiply_fusion
  495.8 2.2 reshape_reshape.3
  498.0 1.8 reverse_bitcast_fusion
  499.8 2.5 copy.34
  502.3 1.2 copy.38
  503.5 0.9 copy.35
  504.5 0.2 maximum_select_fusion.1
  504.7 1.1 fusion.11
  505.8 1.0 slice_dynamic-update-slice_fusion.2
  506.8 1.1 fusion.12
  507.9 1.1 fusion.13
  509.0 1.0 slice_dynamic-update-slice_fusion.1
  510.0 1.1 fusion.14
  511.1 1.1 fusion.15
  512.2 1.0 slice_dynamic-update-slice_fusion
  513.2 1.1 fusion.16
  514.2 8.6 %copy.33 = bf16[8,128,2880]{2,1,0:T(8,128)(2,1)} copy(bf16[8,128,2880]{1,2,0:T(8,128)(2,1)} %fusion.16) | data formatting | bytes 11796480 | tf_op jit(solution)/shard_map/concatenate | solution.py:48
  522.8 0.9 concatenate.16
  523.7 0.7 constant_dynamic-slice_fusion
  524.5 5.0 fusion.4
  529.5 0.1 copy.40
  529.6 0.9 copy.36
  530.5 117.5 %all-reduce.8.cloned.1.call-done = bf16[180,320]{1,0:T(8,128)(2,1)} async-done(((bf16[180,320]{1,0:T(8,128)(2,1)}), bf16[180,320]{1,0:T(8,128)(2,1)}) %all-reduce.8.cloned.1.call-update) | async-done | bytes 115216 | tf_op jit(solution)/shard_map/psum | solution.py:112
  648.0 2.0 divide_subtract_fusion
  (42 shorter events, 1.6 us)
Async XLA Ops:
  9.8 114.6 %all-to-all-start = ((bf16[16,180,320]{2,1,0:T(8,128)(2,1)}), bf16[16,180,320]{2,1,0:T(8,128)(2,1)S(1)}, u32[]{:S(2)}, u32[]{:S(2)}) async-start(bf16[16,180,320]{2,1,0:T(8,128)(2,1)} %stack.2), calls=%async_computation | async-start | bytes 4521984 | tf_op jit(solution)/shard_map/all_to_all | solution.py:73
  25.6 622.4 %all-reduce.8.cloned.1.call-start = ((), (), s32[]{:S(2)}) async-start(), calls=%async_computation.1 | async-start | bytes 282624 | tf_op jit(solution)/shard_map/psum | solution.py:112
  27.5 10.5 %collective-permute-start = (bf16[1,128,320]{1,2,0:T(8,128)(2,1)S(1)}, bf16[1,128,320]{1,2,0:T(8,128)(2,1)S(1)}, u32[]{:S(2)}, u32[]{:S(2)}) collective-permute-start(bf16[1,128,320]{1,2,0:T(8,128)(2,1)S(1)} %get-tuple-element.46), channel_id=1, source_target_pairs={{16,0},{32,16},{48,32},{64,48},{80,64},{96,80},{112,96},{128,112},... | collective-permute-start | bytes 245768 | tf_op jit(solution)/shard_map/ppermute | solution.py:20
  30.4 7.7 %collective-permute-start.1 = (bf16[1,128,320]{1,2,0:T(8,128)(2,1)S(1)}, bf16[1,128,320]{1,2,0:T(8,128)(2,1)S(1)}, u32[]{:S(2)}, u32[]{:S(2)}) collective-permute-start(bf16[1,128,320]{1,2,0:T(8,128)(2,1)S(1)} %get-tuple-element.47), channel_id=1, source_target_pairs={{0,16},{16,32},{32,48},{48,64},{64,80},{80,96},{96,112},{112,128},... | collective-permute-start | bytes 245768 | tf_op jit(solution)/shard_map/ppermute | solution.py:18
  126.7 139.3 %copy-start.4 = (f32[320]{0:T(512)S(1)}, f32[320]{0:T(512)}, u32[]{:S(2)}) copy-start(f32[320]{0:T(512)} %param.12) | copy-start | bytes 3844
  126.7 139.3 %copy-start.5 = (f32[320]{0:T(512)S(1)}, f32[320]{0:T(512)}, u32[]{:S(2)}) copy-start(f32[320]{0:T(512)} %param.13) | copy-start | bytes 3844
  380.6 142.2 %collective-permute-start.4 = (bf16[180,320]{1,0:T(8,128)(2,1)S(1)}, bf16[180,320]{1,0:T(8,128)(2,1)S(1)}, u32[]{:S(2)}, u32[]{:S(2)}) collective-permute-start(bf16[180,320]{1,0:T(8,128)(2,1)S(1)} %slice.98), channel_id=1, source_target_pairs={{0,1},{1,2},{2,3},{3,4},{4,5},{5,6},{6,7},{7,8},{8,9},{9,10},{10,1... | collective-permute-start | bytes 345608
  383.3 121.2 %collective-permute-start.3 = (bf16[1,128,320]{1,2,0:T(8,128)(2,1)}, bf16[1,128,320]{1,2,0:T(8,128)(2,1)S(1)}, u32[]{:S(2)}, u32[]{:S(2)}) collective-permute-start(bf16[1,128,320]{1,2,0:T(8,128)(2,1)} %constant_dynamic-slice_fusion.1), channel_id=1, source_target_pairs={{0,16},{16,32},{32,48},{48,64},{64,80},{80,96},{96,112},{112,128},... | collective-permute-start | bytes 245768 | tf_op jit(solution)/shard_map/ppermute | solution.py:18
  388.6 115.9 %collective-permute-start.2 = (bf16[1,128,320]{1,2,0:T(8,128)(2,1)}, bf16[1,128,320]{1,2,0:T(8,128)(2,1)S(1)}, u32[]{:S(2)}, u32[]{:S(2)}) collective-permute-start(bf16[1,128,320]{1,2,0:T(8,128)(2,1)} %slice_bitcast_fusion), channel_id=1, source_target_pairs={{16,0},{32,16},{48,32},{64,48},{80,64},{96,80},{112,96},{128,112},... | collective-permute-start | bytes 245768 | tf_op jit(solution)/shard_map/ppermute | solution.py:20
  514.2 10.2 %copy-start = (bf16[9,320,320]{2,1,0:T(8,128)(2,1)S(1)}, bf16[9,320,320]{2,1,0:T(8,128)(2,1)}, u32[]{:S(2)}) copy-start(bf16[9,320,320]{2,1,0:T(8,128)(2,1)} %copy.34) | copy-start | bytes 5529604
  529.4 118.6 %copy-start.1 = (f32[180,320]{1,0:T(8,128)S(1)}, f32[180,320]{1,0:T(8,128)}, u32[]{:S(2)}) copy-start(f32[180,320]{1,0:T(8,128)} %param.11) | copy-start | bytes 691204
  529.4 118.6 %copy-start.2 = (f32[180,320]{1,0:T(8,128)S(1)}, f32[180,320]{1,0:T(8,128)}, u32[]{:S(2)}) copy-start(f32[180,320]{1,0:T(8,128)} %param.14) | copy-start | bytes 691204
  529.4 118.5 %copy-start.3 = (f32[180,320]{1,0:T(8,128)S(1)}, f32[180,320]{1,0:T(8,128)}, u32[]{:S(2)}) copy-start(f32[180,320]{1,0:T(8,128)} %param.15) | copy-start | bytes 691204
Sparse Core Ops, SparseCore 0:
  524.6 123.3 all-reduce.7
